TPU v7x, 256 devices: a whole 4x4x8 slice. The times are simulated.
256 devices in a mesh: section: 64 (over z_hi, y, x, core), tp: 4 (over z_lo).
Axes of the slice: x: 4, y: 4, z: 8 (z_hi: 2, z_lo: 4; z = z_hi * 4 + z_lo), core: 2. Of those that a mesh axis runs over, the one named last changes fastest.
Arguments:
- param: float32 [4096, 3584], P('section', 'tp'), may hold values from -4 to 4
- moment_one: float32 [4096, 3584], P('section', 'tp'), may hold values from -2 to 2
- moment_two: float32 [4096, 3584], P('section', 'tp'), may hold values from 0.001 to 1
- proj_grad: float32 [4096, 3584], P('section', 'tp'), may hold values from -6 to 6
- embed_grad: bfloat16 [32768, 3584], P('section', 'tp'), may hold values from -6 to 6
- token_ids: int32 [32768], P('section'), may hold values from 0 to 4095, as said below
- next_ids: int32 [32768], P('section'), may hold values from 0 to 4095, as said below
Outputs:
- new_param: float32 [4096, 3584], P('section', 'tp')
- new_moment_one: float32 [4096, 3584], P('section', 'tp')
- new_moment_two: float32 [4096, 3584], P('section', 'tp')
- next_rows: bfloat16 [32768, 3584], P('section')
Inputs may be any that keep to these rules, and one draw needn't show every extreme that they name: `token_ids`: in each section index's block of 512 tokens at most 16 ids fall into any one owner's run of 64 table rows (id // 64); in every draw some owner receives exactly 16 from every block. `next_ids`: the same bound of 16 a block and an owner holds, and is reached, as for token_ids.
All inputs are finite; a program needn't handle non-finite values.
Results may differ from a plain program's by a relative error of at most 0.001.
Values may be sent and summed in bfloat16 or wider, within the bound.
No kernel may reach another device: no remote copies, remote signals or barrier semaphores. Data moves between devices by JAX's collectives and lax.ppermute only.
A program may use at most 64 MiB of HBM per device.

v0:
```python
import jax
import jax.numpy as jnp
from jax import lax
from jax.sharding import PartitionSpec as P

STEP = 1000


def slot_layout(ids, owners, cap, rows_own):
    owner = ids // rows_own
    hits = (owner[:, None] == jnp.arange(owners)[None, :]).astype(jnp.int32)
    before = jnp.cumsum(hits, axis=0) - hits
    rank = jnp.sum(before * hits, axis=1)
    return (owner * cap + rank, ids - owner * rows_own)


def on_device(param, moment_one, moment_two, proj_grad, embed_grad, token_ids, next_ids):
    rows_own, width = param.shape
    owners = lax.axis_size("section")
    tokens_here = token_ids.shape[0]
    cap = 2 * tokens_here // owners
    slot, local = slot_layout(token_ids, owners, cap, rows_own)
    outgoing = jnp.zeros((owners * cap, width), jnp.bfloat16).at[slot].set(embed_grad)
    targets = jnp.full((owners * cap,), -1, jnp.int32).at[slot].set(local)
    got_rows, got_local = (
        lax.all_to_all(
            outgoing.reshape(owners, cap, width), "section", split_axis=0, concat_axis=0, tiled=True
        ),
        lax.all_to_all(
            targets.reshape(owners, cap), "section", split_axis=0, concat_axis=0, tiled=True
        ),
    )
    select = (jnp.arange(rows_own)[:, None] == got_local.reshape(-1)[None, :]).astype(jnp.bfloat16)
    embed_sum = jnp.dot(
        select, got_rows.reshape(owners * cap, width), preferred_element_type=jnp.float32
    )
    grad = proj_grad + embed_sum
    new_moment_one = 0.9 * moment_one + 0.1 * grad
    new_moment_two = 0.999 * moment_two + 0.001 * grad * grad
    first_fix = 1.0 - 0.9**STEP
    second_fix = 1.0 - 0.999**STEP
    new_param = param - 0.01 * (new_moment_one / first_fix) / (
        jnp.sqrt(new_moment_two / second_fix) + 1e-08
    )
    table = new_param.astype(jnp.bfloat16)
    slot, local = slot_layout(next_ids, owners, cap, rows_own)
    asking = jnp.full((owners * cap,), -1, jnp.int32).at[slot].set(local).reshape(owners, cap)
    found = jnp.take(
        table,
        jnp.clip(
            lax.all_to_all(asking, "section", split_axis=0, concat_axis=0, tiled=True),
            0,
            rows_own - 1,
        ),
        axis=0,
    )
    replies = lax.all_to_all(found, "section", split_axis=0, concat_axis=0, tiled=True)
    mine = jnp.take(replies.reshape(owners * cap, width), slot, axis=0)
    next_rows = lax.all_gather(mine, "tp", axis=1, tiled=True)
    return (new_param, new_moment_one, new_moment_two, next_rows)


def solution(mesh):
    placed = (
        P("section", "tp"),
        P("section", "tp"),
        P("section", "tp"),
        P("section", "tp"),
        P("section", "tp"),
        P("section"),
        P("section"),
    )
    return jax.shard_map(
        on_device,
        mesh=mesh,
        in_specs=placed,
        out_specs=(P("section", "tp"), P("section", "tp"), P("section", "tp"), P("section", None)),
        check_vma=False,
    )
```

profile of v0, /device:TPU:1, one launch (start us, length us, event | category | flops | bytes accessed | tf_op | source)
XLA Modules:
  0.0 256.6 jit_solution(6298130976324283758)
XLA Ops:
  7.2 0.7 multiply_subtract_fusion
  7.9 1.2 reduce-window.16
  9.1 0.2 slice_reduce_fusion
  9.4 0.1 fusion.5
  9.5 2.4 scatter_custom_fusion.2
  11.9 0.7 all_to_all.21
  12.6 15.6 %all-to-all-start.2 = ((s32[64,1,16]{2,1,0:T(1,128)}), s32[64,1,16]{2,1,0:T(1,128)S(1)}, u32[]{:S(2)}, u32[]{:S(2)}) async-start(s32[64,1,16]{2,1,0:T(1,128)} %bitcast.7), calls=%async_computation.2 | async-start | bytes 65536 | tf_op jit(solution)/shard_map/all_to_all | solution.py:51
  28.3 0.7 multiply_subtract_fusion.1
  29.0 1.2 reduce-window.14
  30.2 0.2 slice_reduce_fusion.1
  30.4 0.1 fusion.8
  30.6 2.4 scatter_custom_fusion
  33.0 0.7 all_to_all.18
  33.7 6.2 %all-to-all-done.2 = s32[64,1,16]{2,1,0:T(1,128)S(1)} async-done(((s32[64,1,16]{2,1,0:T(1,128)}), s32[64,1,16]{2,1,0:T(1,128)S(1)}, u32[]{:S(2)}, u32[]{:S(2)}) %all-to-all-start.2) | async-done | bytes 4128 | tf_op jit(solution)/shard_map/all_to_all | solution.py:51
  40.0 6.6 %all-to-all-start = ((s32[64,1,16]{2,1,0:T(1,128)}), s32[64,1,16]{2,1,0:T(1,128)S(1)}, u32[]{:S(2)}, u32[]{:S(2)}) async-start(s32[64,1,16]{2,1,0:T(1,128)} %bitcast.2), calls=%async_computation | async-start | bytes 65536 | tf_op jit(solution)/shard_map/all_to_all | solution.py:29
  46.5 4.6 %scatter_custom_fusion.1 = bf16[1024,896]{1,0:T(8,128)(2,1)} fusion(s32[512]{0:T(512)S(1)} %compare_select_fusion.3, bf16[512,896]{1,0:T(8,128)(2,1)} %param.11, bf16[]{:T(256)} %constant.74.clone.1), kind=kCustom, calls=%fused_computation.7 | custom fusion | bytes 1835520 | tf_op jit(solution)/shard_map/scatter | solution.py:23
  51.1 7.1 %all-to-all-done = s32[64,1,16]{2,1,0:T(1,128)S(1)} async-done(((s32[64,1,16]{2,1,0:T(1,128)}), s32[64,1,16]{2,1,0:T(1,128)S(1)}, u32[]{:S(2)}, u32[]{:S(2)}) %all-to-all-start) | async-done | bytes 4128 | tf_op jit(solution)/shard_map/all_to_all | solution.py:29
  58.3 0.0 copy-start
  58.3 0.0 copy-start.1
  58.3 0.0 copy-start.2
  58.3 0.0 copy-start.3
  58.3 5.8 %all-to-all-start.1 = ((bf16[64,16,896]{2,1,0:T(8,128)(2,1)}), bf16[64,16,896]{2,1,0:T(8,128)(2,1)S(1)}, u32[]{:S(2)}, u32[]{:S(2)}) async-start(bf16[64,16,896]{2,1,0:T(8,128)(2,1)} %bitcast.56), calls=%async_computation.1 | async-start | bytes 3670016 | tf_op jit(solution)/shard_map/all_to_all | solution.py:26
  64.2 0.1 reshape.102
  64.3 0.5 broadcast.142
  64.8 0.7 reduce.7
  65.5 0.1 eq.69
  65.6 32.1 %all-to-all-done.1 = bf16[64,16,896]{2,1,0:T(8,128)(2,1)S(1)} async-done(((bf16[64,16,896]{2,1,0:T(8,128)(2,1)}), bf16[64,16,896]{2,1,0:T(8,128)(2,1)S(1)}, u32[]{:S(2)}, u32[]{:S(2)}) %all-to-all-start.1) | async-done | bytes 1835040 | tf_op jit(solution)/shard_map/all_to_all | solution.py:26
  97.7 0.0 copy-done
  97.7 0.0 copy-done.1
  97.7 0.0 copy-done.2
  97.7 0.0 copy-done.3
  97.7 1.3 fusion.20
  99.1 4.0 %gather_fusion = bf16[1024,896]{1,0:T(8,128)(2,1)S(1)} fusion(bf16[64,896]{1,0:T(8,128)(2,1)S(1)} %get-tuple-element.8, s32[1024]{0:T(1024)S(1)} %broadcast_clamp_fusion.1), kind=kCustom, calls=%fused_computation | custom fusion | bytes 3674112 | tf_op jit(solution)/shard_map/jit(_take)/gather | solution.py:48
  103.1 1.5 broadcast_select_fusion
  104.6 19.2 %all-to-all-start.3 = ((bf16[64,16,896]{2,1,0:T(8,128)(2,1)}), bf16[64,16,896]{2,1,0:T(8,128)(2,1)S(1)}, u32[]{:S(2)}, u32[]{:S(2)}) async-start(bf16[64,16,896]{2,1,0:T(8,128)(2,1)} %broadcast_select_fusion), calls=%async_computation.3 | async-start | bytes 3670016 | tf_op jit(solution)/shard_map/all_to_all | solution.py:57
  123.8 0.0 all-gather.2.cloned.1.call-start
  123.9 28.8 %all-to-all-done.3 = bf16[64,16,896]{2,1,0:T(8,128)(2,1)S(1)} async-done(((bf16[64,16,896]{2,1,0:T(8,128)(2,1)}), bf16[64,16,896]{2,1,0:T(8,128)(2,1)S(1)}, u32[]{:S(2)}, u32[]{:S(2)}) %all-to-all-start.3) | async-done | bytes 1835040 | tf_op jit(solution)/shard_map/all_to_all | solution.py:57
  152.7 2.0 gather_fusion.1
  154.7 1.1 broadcast_select_fusion.1
  155.8 0.0 all-gather.2.cloned.1.call-update
  155.9 89.8 %all-gather.2.cloned.1.call-done = bf16[512,3584]{1,0:T(8,128)(2,1)} async-done(((bf16[512,896]{1,0:T(8,128)(2,1)}), bf16[512,3584]{1,0:T(8,128)(2,1)}) %all-gather.2.cloned.1.call-update) | async-done | bytes 3670032 | tf_op jit(solution)/shard_map/all_gather | solution.py:59
  245.7 4.1 %copy.22 = bf16[512,3584]{1,0:T(8,128)(2,1)} copy(bf16[512,3584]{1,0:T(8,128)(2,1)} %all-gather.2.cloned.1.call-done) | data formatting | bytes 7340032
  (13 shorter events, 0.2 us)
Async XLA Ops:
  12.6 27.3 %all-to-all-start.2 = ((s32[64,1,16]{2,1,0:T(1,128)}), s32[64,1,16]{2,1,0:T(1,128)S(1)}, u32[]{:S(2)}, u32[]{:S(2)}) async-start(s32[64,1,16]{2,1,0:T(1,128)} %bitcast.7), calls=%async_computation.2 | async-start | bytes 65536 | tf_op jit(solution)/shard_map/all_to_all | solution.py:51
  40.0 18.3 %all-to-all-start = ((s32[64,1,16]{2,1,0:T(1,128)}), s32[64,1,16]{2,1,0:T(1,128)S(1)}, u32[]{:S(2)}, u32[]{:S(2)}) async-start(s32[64,1,16]{2,1,0:T(1,128)} %bitcast.2), calls=%async_computation | async-start | bytes 65536 | tf_op jit(solution)/shard_map/all_to_all | solution.py:29
  58.3 39.4 %copy-start = (f32[64,896]{1,0:T(8,128)S(1)}, f32[64,896]{1,0:T(8,128)}, u32[]{:S(2)}) copy-start(f32[64,896]{1,0:T(8,128)} %param.7) | copy-start | bytes 688132
  58.3 39.4 %copy-start.1 = (f32[64,896]{1,0:T(8,128)S(1)}, f32[64,896]{1,0:T(8,128)}, u32[]{:S(2)}) copy-start(f32[64,896]{1,0:T(8,128)} %param.8) | copy-start | bytes 688132
  58.3 39.4 %copy-start.2 = (f32[64,896]{1,0:T(8,128)S(1)}, f32[64,896]{1,0:T(8,128)}, u32[]{:S(2)}) copy-start(f32[64,896]{1,0:T(8,128)} %param.9) | copy-start | bytes 688132
  58.3 39.4 %copy-start.3 = (f32[64,896]{1,0:T(8,128)S(1)}, f32[64,896]{1,0:T(8,128)}, u32[]{:S(2)}) copy-start(f32[64,896]{1,0:T(8,128)} %param.10) | copy-start | bytes 688132
  58.3 39.4 %all-to-all-start.1 = ((bf16[64,16,896]{2,1,0:T(8,128)(2,1)}), bf16[64,16,896]{2,1,0:T(8,128)(2,1)S(1)}, u32[]{:S(2)}, u32[]{:S(2)}) async-start(bf16[64,16,896]{2,1,0:T(8,128)(2,1)} %bitcast.56), calls=%async_computation.1 | async-start | bytes 3670016 | tf_op jit(solution)/shard_map/all_to_all | solution.py:26
  104.6 48.0 %all-to-all-start.3 = ((bf16[64,16,896]{2,1,0:T(8,128)(2,1)}), bf16[64,16,896]{2,1,0:T(8,128)(2,1)S(1)}, u32[]{:S(2)}, u32[]{:S(2)}) async-start(bf16[64,16,896]{2,1,0:T(8,128)(2,1)} %broadcast_select_fusion), calls=%async_computation.3 | async-start | bytes 3670016 | tf_op jit(solution)/shard_map/all_to_all | solution.py:57
  123.8 121.8 %all-gather.2.cloned.1.call-start = ((), (), s32[]{:S(2)}) async-start(), calls=%async_computation.4 | async-start | bytes 4587520 | tf_op jit(solution)/shard_map/all_gather | solution.py:59
Sparse Core Ops, SparseCore 0:
  156.0 89.6 all-gather.1
where the time goes:
time: 257 us
  waiting for transfers between devices  164 us (64%)
  starting transfers between devices  47.2 us (18%)
  local copies, waits for them, and re-layouts  22.2 us (9%)
  between operations  14.2 us (6%)
  other arithmetic  7.61 us (3%)
    all_gather x1, waiting for transfers between devices, on_device(): next_rows = lax.all_gather(mine, 'tp', axis=1, tiled=True)  89.8 us
    all_to_all x1, waiting for transfers between devices, on_device(): lax.all_to_all(outgoing.reshape(owners, cap, width), 'section', split_axi...  32.1 us
    all_to_all x1, waiting for transfers between devices, on_device(): lax.all_to_all(found, 'section', split_axis=0, concat_axis=0, tiled=True)  28.8 us
    all_to_all x1, starting transfers between devices, on_device(): lax.all_to_all(found, 'section', split_axis=0, concat_axis=0, tiled=True)  19.2 us
    all_to_all x1, starting transfers between devices, on_device(): lax.all_to_all(asking, 'section', split_axis=0, concat_axis=0, tiled=True)  15.6 us
    all_to_all x1, waiting for transfers between devices, on_device(): lax.all_to_all(targets.reshape(owners, cap), 'section', split_axis=0, con...  7.12 us
    all_to_all x1, starting transfers between devices, on_device(): lax.all_to_all(targets.reshape(owners, cap), 'section', split_axis=0, con...  6.58 us
    all_to_all x1, waiting for transfers between devices, on_device(): lax.all_to_all(asking, 'section', split_axis=0, concat_axis=0, tiled=True)  6.23 us
  transfers between devices with their start and end apart: 5, of which 5 were waited for; matrix products, arithmetic and copies ran while one was open for 4% of the time, Pallas kernels for 0%

commit v1 on v0

--- a/solution.py
+++ b/solution.py
@@ -2,6 +2,7 @@
 import jax.numpy as jnp
 from jax import lax
 from jax.sharding import PartitionSpec as P
+from jax.lax import all_to_all, axis_size
 
 STEP = 1000
 
@@ -56,7 +57,12 @@
     )
     replies = lax.all_to_all(found, "section", split_axis=0, concat_axis=0, tiled=True)
     mine = jnp.take(replies.reshape(owners * cap, width), slot, axis=0)
-    next_rows = lax.all_gather(mine, "tp", axis=1, tiled=True)
+    next_rows = jnp.concatenate(
+        all_to_all(
+            jnp.stack(axis_size("tp") * [mine]), split_axis=0, axis_name="tp", concat_axis=0
+        ),
+        axis=1,
+    )
     return (new_param, new_moment_one, new_moment_two, next_rows)
 
 

time: 257 us -> 265 us (1.031)
  blocking collectives: 0 us -> 104 us
  waiting for transfers between devices: 164 us -> 74.3 us
  between operations: 14.2 us -> 0.8 us
  local copies, waits for them, and re-layouts: 22.2 us -> 30.2 us
    all_to_all x0 -> x1, blocking collectives: none -> 104 us  [on_device(): all_to_all(jnp.stack(axis_size('tp') * [mine]), split_axis=0, axis_name='...]
    all_gather x1 -> x0, waiting for transfers between devices: 89.8 us -> none  [on_device(): next_rows = lax.all_gather(mine, 'tp', axis=1, tiled=True)]
    all_to_all x0 -> x1, local copies, waits for them, and re-layouts: none -> 5.94 us  [on_device(): all_to_all(jnp.stack(axis_size('tp') * [mine]), split_axis=0, axis_name='...]
  transfers between devices with their start and end apart: 5 -> 4, of which waited for: 5 -> 4; matrix products, arithmetic and copies ran while one was open for 4% -> 4% of each run, Pallas kernels for 0% -> 0%
where the time goes in v1:
time: 265 us; the launch traced here: 264 us
  blocking collectives  104 us (39%)
  waiting for transfers between devices  74.3 us (28%)
  starting transfers between devices  47.2 us (18%)
  local copies, waits for them, and re-layouts  30.2 us (11%)
  other arithmetic  6.68 us (3%)
    all_to_all x1, blocking collectives, on_device(): all_to_all(jnp.stack(axis_size('tp') * [mine]), split_axis=0, axis_name='...  104 us
    all_to_all x1, waiting for transfers between devices, on_device(): lax.all_to_all(outgoing.reshape(owners, cap, width), 'section', split_axi...  32.1 us
    all_to_all x1, waiting for transfers between devices, on_device(): lax.all_to_all(found, 'section', split_axis=0, concat_axis=0, tiled=True)  28.9 us
    all_to_all x1, starting transfers between devices, on_device(): lax.all_to_all(found, 'section', split_axis=0, concat_axis=0, tiled=True)  19.2 us
    all_to_all x1, starting transfers between devices, on_device(): lax.all_to_all(asking, 'section', split_axis=0, concat_axis=0, tiled=True)  15.6 us
    all_to_all x1, waiting for transfers between devices, on_device(): lax.all_to_all(targets.reshape(owners, cap), 'section', split_axis=0, con...  7.12 us
    all_to_all x1, starting transfers between devices, on_device(): lax.all_to_all(targets.reshape(owners, cap), 'section', split_axis=0, con...  6.58 us
    all_to_all x1, waiting for transfers between devices, on_device(): lax.all_to_all(asking, 'section', split_axis=0, concat_axis=0, tiled=True)  6.23 us
  transfers between devices with their start and end apart: 4, of which 4 were waited for; matrix products, arithmetic and copies ran while one was open for 4% of the time, Pallas kernels for 0%

profile of v1, /device:TPU:1, one launch (start us, length us, event | category | flops | bytes accessed | tf_op | source)
XLA Modules:
  0.0 264.2 jit_solution(14296244771460653751)
XLA Ops:
  0.6 0.7 multiply_subtract_fusion
  1.3 1.2 reduce-window.16
  2.5 0.2 slice_reduce_fusion
  2.8 0.1 fusion.5
  3.0 2.4 scatter_custom_fusion.2
  5.4 0.7 all_to_all.24
  6.1 15.6 %all-to-all-start.2 = ((s32[64,1,16]{2,1,0:T(1,128)}), s32[64,1,16]{2,1,0:T(1,128)S(1)}, u32[]{:S(2)}, u32[]{:S(2)}) async-start(s32[64,1,16]{2,1,0:T(1,128)} %bitcast.7), calls=%async_computation.2 | async-start | bytes 65536 | tf_op jit(solution)/shard_map/all_to_all | solution.py:52
  21.7 0.7 multiply_subtract_fusion.1
  22.4 1.2 reduce-window.14
  23.6 0.2 slice_reduce_fusion.1
  23.9 0.1 fusion.8
  24.0 2.4 scatter_custom_fusion
  26.5 0.7 all_to_all.21
  27.2 6.2 %all-to-all-done.2 = s32[64,1,16]{2,1,0:T(1,128)S(1)} async-done(((s32[64,1,16]{2,1,0:T(1,128)}), s32[64,1,16]{2,1,0:T(1,128)S(1)}, u32[]{:S(2)}, u32[]{:S(2)}) %all-to-all-start.2) | async-done | bytes 4128 | tf_op jit(solution)/shard_map/all_to_all | solution.py:52
  33.4 6.6 %all-to-all-start = ((s32[64,1,16]{2,1,0:T(1,128)}), s32[64,1,16]{2,1,0:T(1,128)S(1)}, u32[]{:S(2)}, u32[]{:S(2)}) async-start(s32[64,1,16]{2,1,0:T(1,128)} %bitcast.2), calls=%async_computation | async-start | bytes 65536 | tf_op jit(solution)/shard_map/all_to_all | solution.py:30
  40.0 4.6 %scatter_custom_fusion.1 = bf16[1024,896]{1,0:T(8,128)(2,1)} fusion(s32[512]{0:T(512)S(1)} %compare_select_fusion.3, bf16[512,896]{1,0:T(8,128)(2,1)} %param.11, bf16[]{:T(256)} %constant.74.clone.1), kind=kCustom, calls=%fused_computation.7 | custom fusion | bytes 1835520 | tf_op jit(solution)/shard_map/scatter | solution.py:24
  44.6 7.1 %all-to-all-done = s32[64,1,16]{2,1,0:T(1,128)S(1)} async-done(((s32[64,1,16]{2,1,0:T(1,128)}), s32[64,1,16]{2,1,0:T(1,128)S(1)}, u32[]{:S(2)}, u32[]{:S(2)}) %all-to-all-start) | async-done | bytes 4128 | tf_op jit(solution)/shard_map/all_to_all | solution.py:30
  51.7 0.0 copy-start
  51.7 0.0 copy-start.1
  51.7 0.0 copy-start.2
  51.7 0.0 copy-start.3
  51.7 5.8 %all-to-all-start.1 = ((bf16[64,16,896]{2,1,0:T(8,128)(2,1)}), bf16[64,16,896]{2,1,0:T(8,128)(2,1)S(1)}, u32[]{:S(2)}, u32[]{:S(2)}) async-start(bf16[64,16,896]{2,1,0:T(8,128)(2,1)} %bitcast.60), calls=%async_computation.1 | async-start | bytes 3670016 | tf_op jit(solution)/shard_map/all_to_all | solution.py:27
  57.6 0.1 reshape.118
  57.7 0.5 broadcast.147
  58.2 0.7 reduce.7
  59.0 0.1 eq.69
  59.1 32.1 %all-to-all-done.1 = bf16[64,16,896]{2,1,0:T(8,128)(2,1)S(1)} async-done(((bf16[64,16,896]{2,1,0:T(8,128)(2,1)}), bf16[64,16,896]{2,1,0:T(8,128)(2,1)S(1)}, u32[]{:S(2)}, u32[]{:S(2)}) %all-to-all-start.1) | async-done | bytes 1835040 | tf_op jit(solution)/shard_map/all_to_all | solution.py:27
  91.2 0.0 copy-done
  91.2 0.0 copy-done.1
  91.2 0.0 copy-done.2
  91.2 0.0 copy-done.3
  91.2 1.3 fusion.20
  92.5 4.0 %gather_fusion = bf16[1024,896]{1,0:T(8,128)(2,1)S(1)} fusion(bf16[64,896]{1,0:T(8,128)(2,1)S(1)} %get-tuple-element.12, s32[1024]{0:T(1024)S(1)} %broadcast_clamp_fusion.1), kind=kCustom, calls=%fused_computation | custom fusion | bytes 3674112 | tf_op jit(solution)/shard_map/jit(_take)/gather | solution.py:49
  96.6 1.5 broadcast_select_fusion
  98.1 19.2 %all-to-all-start.3 = ((bf16[64,16,896]{2,1,0:T(8,128)(2,1)}), bf16[64,16,896]{2,1,0:T(8,128)(2,1)S(1)}, u32[]{:S(2)}, u32[]{:S(2)}) async-start(bf16[64,16,896]{2,1,0:T(8,128)(2,1)} %broadcast_select_fusion), calls=%async_computation.3 | async-start | bytes 3670016 | tf_op jit(solution)/shard_map/all_to_all | solution.py:58
  117.3 28.9 %all-to-all-done.3 = bf16[64,16,896]{2,1,0:T(8,128)(2,1)S(1)} async-done(((bf16[64,16,896]{2,1,0:T(8,128)(2,1)}), bf16[64,16,896]{2,1,0:T(8,128)(2,1)S(1)}, u32[]{:S(2)}, u32[]{:S(2)}) %all-to-all-start.3) | async-done | bytes 1835040 | tf_op jit(solution)/shard_map/all_to_all | solution.py:58
  146.1 2.0 gather_fusion.1
  148.2 0.2 broadcast_select_fusion.1
  148.4 0.3 stack.2
  148.7 103.7 %all_to_all.33 = bf16[4,512,896]{2,1,0:T(8,128)(2,1)} all-to-all(bf16[4,512,896]{2,1,0:T(8,128)(2,1)S(1)} %stack.2), channel_id=1, replica_groups=mesh['section'=64,'tp'=4] {'tp'}, dimensions={0} | all-to-all | bytes 7340032 | tf_op jit(solution)/shard_map/all_to_all | solution.py:61
  252.3 5.9 %copy.21 = bf16[4,512,896]{1,2,0:T(8,128)(2,1)} copy(bf16[4,512,896]{2,1,0:T(8,128)(2,1)} %all_to_all.33) | data formatting | bytes 7340032 | tf_op jit(solution)/shard_map/all_to_all | solution.py:61
  258.3 5.9 %copy.22 = bf16[512,3584]{1,0:T(8,128)(2,1)} copy(bf16[512,3584]{0,1:T(8,128)(2,1)} %bitcast.58) | data formatting | bytes 7340032
  (13 shorter events, 0.2 us)
Async XLA Ops:
  6.1 27.3 %all-to-all-start.2 = ((s32[64,1,16]{2,1,0:T(1,128)}), s32[64,1,16]{2,1,0:T(1,128)S(1)}, u32[]{:S(2)}, u32[]{:S(2)}) async-start(s32[64,1,16]{2,1,0:T(1,128)} %bitcast.7), calls=%async_computation.2 | async-start | bytes 65536 | tf_op jit(solution)/shard_map/all_to_all | solution.py:52
  33.4 18.3 %all-to-all-start = ((s32[64,1,16]{2,1,0:T(1,128)}), s32[64,1,16]{2,1,0:T(1,128)S(1)}, u32[]{:S(2)}, u32[]{:S(2)}) async-start(s32[64,1,16]{2,1,0:T(1,128)} %bitcast.2), calls=%async_computation | async-start | bytes 65536 | tf_op jit(solution)/shard_map/all_to_all | solution.py:30
  51.7 39.4 %copy-start = (f32[64,896]{1,0:T(8,128)S(1)}, f32[64,896]{1,0:T(8,128)}, u32[]{:S(2)}) copy-start(f32[64,896]{1,0:T(8,128)} %param.7) | copy-start | bytes 688132
  51.7 39.4 %copy-start.1 = (f32[64,896]{1,0:T(8,128)S(1)}, f32[64,896]{1,0:T(8,128)}, u32[]{:S(2)}) copy-start(f32[64,896]{1,0:T(8,128)} %param.8) | copy-start | bytes 688132
  51.7 39.4 %copy-start.2 = (f32[64,896]{1,0:T(8,128)S(1)}, f32[64,896]{1,0:T(8,128)}, u32[]{:S(2)}) copy-start(f32[64,896]{1,0:T(8,128)} %param.9) | copy-start | bytes 688132
  51.7 39.4 %copy-start.3 = (f32[64,896]{1,0:T(8,128)S(1)}, f32[64,896]{1,0:T(8,128)}, u32[]{:S(2)}) copy-start(f32[64,896]{1,0:T(8,128)} %param.10) | copy-start | bytes 688132
  51.7 39.4 %all-to-all-start.1 = ((bf16[64,16,896]{2,1,0:T(8,128)(2,1)}), bf16[64,16,896]{2,1,0:T(8,128)(2,1)S(1)}, u32[]{:S(2)}, u32[]{:S(2)}) async-start(bf16[64,16,896]{2,1,0:T(8,128)(2,1)} %bitcast.60), calls=%async_computation.1 | async-start | bytes 3670016 | tf_op jit(solution)/shard_map/all_to_all | solution.py:27
  98.1 48.0 %all-to-all-start.3 = ((bf16[64,16,896]{2,1,0:T(8,128)(2,1)}), bf16[64,16,896]{2,1,0:T(8,128)(2,1)S(1)}, u32[]{:S(2)}, u32[]{:S(2)}) async-start(bf16[64,16,896]{2,1,0:T(8,128)(2,1)} %broadcast_select_fusion), calls=%async_computation.3 | async-start | bytes 3670016 | tf_op jit(solution)/shard_map/all_to_all | solution.py:58
